TPU v7x, 32 devices: a whole 2x2x4 slice. The times are simulated.
32 devices in a mesh: grp: 2 (over y), gz: 4 (over z), gy: 2 (over x), sa: 2 (over core).
Axes of the slice: x: 2, y: 2, z: 4, core: 2. Of those that a mesh axis runs over, the one named last changes fastest.
Arguments:
- field: float32 [8, 32, 16, 128], P('sa', ('grp', 'gz'), 'gy'), parts along dimension 1, may hold values from 0 to 2
- diffusion: float32 [8], P('sa'), may hold values from 0.02 to 0.16
- secrete: float32 [8, 65536], P('sa', ('grp', 'gz', 'gy')), parts along dimension 1, may hold values from 0 to 1
- uptake: float32 [8, 65536], P('sa', ('grp', 'gz', 'gy')), parts along dimension 1, may hold values from 0.05 to 1
- cell_voxel: int32 [65536], P(('grp', 'gz', 'gy')), parts along dimension 0, may hold values from 0 to 4095
- block_dest: int32 [512, 1], P(('grp', 'gz', 'gy')), parts along dimension 0, may hold values from 0 to 3; in each aligned block of 32 rows (0 to 31, 32 to 63, ...) at most 24 rows name the same one
Outputs:
- new_field: float32 [8, 32, 16, 128], P('sa', ('grp', 'gz'), 'gy'), parts along dimension 1
- cell_conc: float32 [8, 65536], P('sa', ('grp', 'gz', 'gy')), parts along dimension 1
There are 2 independent parts, one for each index of `grp`. A program takes and returns all parts, laid end to end along the dimension named above; an argument that names none is the same for every part. Nothing has to cross between parts.
Inputs may be any that keep to these rules, and one draw needn't show every extreme that they name: `block_dest`: among the 32 blocks of one device at most 24 name the same destination, and in every draw some device has exactly 24 blocks naming one destination.
All inputs are finite; a program needn't handle non-finite values.
Results may differ from a plain program's by a relative error of at most 0.00007.
Values sent between devices are 32-bit elements; how exact they have to be, the bound alone decides.
A program may use at most 64 MiB of HBM per device.

v0:
```python
import math

import jax
import jax.numpy as jnp
from jax import lax
from jax.sharding import PartitionSpec as P

HIGH = lax.Precision.HIGHEST


def extended(block, sides, width):
    for axis, dim in sides:
        count = lax.axis_size(axis)
        forward = [(i, i + 1) for i in range(count - 1)]
        backward = [(target, source) for source, target in forward]
        low = lax.ppermute(
            lax.slice_in_dim(block, block.shape[dim] - width, None, axis=dim), axis, forward
        )
        high = lax.ppermute(lax.slice_in_dim(block, 0, width, axis=dim), axis, backward)
        block = jnp.concatenate([low, block, high], axis=dim)
    return block


def neighbours(padded):
    beside_all = padded[:, 2:, 1:-1, 1:-1] + padded[:, :-2, 1:-1, 1:-1]
    beside_all = beside_all + padded[:, 1:-1, 2:, 1:-1] + padded[:, 1:-1, :-2, 1:-1]
    return beside_all + padded[:, 1:-1, 1:-1, 2:] + padded[:, 1:-1, 1:-1, :-2]


def diffuse(field, diffusion):
    padded = extended(field, (("gz", 1), ("gy", 2)), 1)
    padded = jnp.pad(padded, ((0, 0), (0, 0), (0, 0), (1, 1)))
    return field + diffusion[:, None, None, None] * (neighbours(padded) - 6.0 * field)


def group_size(block_count, per_block):
    return math.gcd(block_count, max(1, 512 // per_block))


def one_hots(voxel_group, highs, lanes):
    high_ids = jnp.arange(highs, dtype=jnp.int32)
    lane_ids = jnp.arange(lanes, dtype=jnp.int32)
    onehot_high = ((voxel_group // lanes)[..., None] == high_ids).astype(jnp.float32)
    onehot_low = ((voxel_group % lanes)[..., None] == lane_ids).astype(jnp.float32)
    return (onehot_high, onehot_low)


def block_sums(values, voxel, highs, lanes, combine, init):
    quantities, block_count, per_block = values.shape
    group = group_size(block_count, per_block)
    steps_count = block_count // group
    grouped_vals = values.reshape(quantities, steps_count, group, per_block).transpose(1, 0, 2, 3)
    grouped_vox = voxel.reshape(steps_count, group, per_block)

    def step(carry, item):
        vals_group, vox_group, step_id = item
        onehot_high, onehot_low = one_hots(vox_group, highs, lanes)
        weighted = vals_group[:, :, :, None] * onehot_low[None]
        part = jnp.einsum("gch,qgcl->gqhl", onehot_high, weighted, precision=HIGH)
        return (combine(carry, part, step_id * group, group), None)

    result, unused = lax.scan(
        step, init, (grouped_vals, grouped_vox, jnp.arange(steps_count, dtype=jnp.int32))
    )
    return result


def block_reads(table_for, voxel, substrates, highs, lanes):
    block_count, per_block = voxel.shape
    group = group_size(block_count, per_block)
    steps_count = block_count // group
    grouped_vox = voxel.reshape(steps_count, group, per_block)

    def step(carry, item):
        vox_group, step_id = item
        onehot_high, onehot_low = one_hots(vox_group, highs, lanes)
        table = table_for(step_id * group, group)
        picked = jnp.einsum("gch,shl->gscl", onehot_high, table, precision=HIGH)
        return (carry, jnp.sum(picked * onehot_low[:, None], axis=3))

    unused, reads = lax.scan(step, 0, (grouped_vox, jnp.arange(steps_count, dtype=jnp.int32)))
    return reads.transpose(2, 0, 1, 3).reshape(substrates, block_count, per_block)


def deposit(secrete, uptake, cell_voxel, block_dest, voxels, lanes):
    substrates = secrete.shape[0]
    blocks = block_dest.shape[0]
    per_block = secrete.shape[1] // blocks
    highs = voxels // lanes
    slab_count = lax.axis_size("gz")
    targets = block_dest[:, 0]
    voxel_blocks = cell_voxel.reshape(blocks, per_block)
    capacity = max(2, 3 * blocks // slab_count)
    block_ids = jnp.arange(blocks, dtype=jnp.int32)
    matches = targets[:, None] == targets[None, :]
    earlier = block_ids[None, :] < block_ids[:, None]
    slot_index = jnp.sum((matches & earlier).astype(jnp.int32), axis=1)
    position = targets * capacity + slot_index
    slots = slab_count * capacity
    placing = (jnp.arange(slots, dtype=jnp.int32)[:, None] == position[None, :]).astype(jnp.float32)
    send_release = jnp.einsum(
        "pb,sbc->spc", placing, secrete.reshape(substrates, blocks, per_block), precision=HIGH
    )
    send_uptake = jnp.einsum(
        "pb,sbc->spc", placing, uptake.reshape(substrates, blocks, per_block), precision=HIGH
    )
    send_index = jnp.dot(placing, voxel_blocks.astype(jnp.float32), precision=HIGH)
    send_index = send_index.astype(jnp.int32).reshape(1, slots, per_block)
    got_release, got_uptake, got_index = (
        lax.all_to_all(send_release, "gz", split_axis=1, concat_axis=1, tiled=True),
        lax.all_to_all(send_uptake, "gz", split_axis=1, concat_axis=1, tiled=True),
        lax.all_to_all(send_index, "gz", split_axis=1, concat_axis=1, tiled=True),
    )
    slot_voxel = got_index.reshape(slots, per_block)
    stacked = jnp.concatenate([got_release, got_uptake], axis=0)

    def add_all(carry, part, first, count):
        return carry + jnp.sum(part, axis=0)

    init = jnp.zeros((2 * substrates, highs, lanes), jnp.float32)
    summed = block_sums(stacked, slot_voxel, highs, lanes, add_all, init).reshape(
        2 * substrates, voxels
    )
    source = summed[:substrates]
    uptake_sum = summed[substrates:]

    def reader(updated):
        table = updated.reshape(substrates, highs, lanes)
        looked_up = block_reads(lambda first, count: table, slot_voxel, substrates, highs, lanes)
        returned = lax.all_to_all(looked_up, "gz", split_axis=1, concat_axis=1, tiled=True)
        back = jnp.einsum("pb,spc->sbc", placing, returned, precision=HIGH)
        return back.reshape(substrates, blocks * per_block)

    return (source, uptake_sum, reader)


def shards(field, diffusion, secrete, uptake, cell_voxel, block_dest):
    substrates = field.shape[0]
    lanes = field.shape[3]
    voxels = field.shape[1] * field.shape[2] * lanes
    source, uptake_sum, reader = deposit(secrete, uptake, cell_voxel, block_dest, voxels, lanes)
    diffused = diffuse(field, diffusion).reshape(substrates, voxels)
    updated = (diffused + source) / (1.0 + uptake_sum)
    cell_conc = reader(updated)
    return (updated.reshape(field.shape), cell_conc)


def solution(mesh):
    in_specs = (
        P("sa", ("grp", "gz"), "gy", None),
        P("sa"),
        P("sa", ("grp", "gz", "gy")),
        P("sa", ("grp", "gz", "gy")),
        P(("grp", "gz", "gy")),
        P(("grp", "gz", "gy"), None),
    )
    out_specs = (P("sa", ("grp", "gz"), "gy", None), P("sa", ("grp", "gz", "gy")))
    return jax.shard_map(shards, mesh=mesh, in_specs=in_specs, out_specs=out_specs, check_vma=False)
```

profile of v0, /device:TPU:0, one launch (start us, length us, event | category | flops | bytes accessed | tf_op | source)
XLA Modules:
  0.0 118.7 jit_solution(11826581008800157441)
XLA Ops:
  2.2 1.2 %convolution_bitcast_fusion = f32[4,96,128]{2,1,0:T(8,128)S(1)} fusion(f32[1,4,32,128]{3,1,2,0:T(4,128)} %bitcast.137, s32[32]{0:T(128)S(1)} %multiply_add_fusion), kind=kOutput, calls=%fused_computation.41 | convolution fusion | flops 18877440 | bytes 262272 | tf_op jit(solution)/shard_map/pb,sbc->spc/dot_general | solution.py:104
  4.2 6.3 %all-to-all-start.1 = ((f32[4,96,128]{2,0,1:T(4,128)}), f32[4,96,128]{2,0,1:T(4,128)S(1)}, u32[]{:S(2)}, u32[]{:S(2)}) async-start(f32[4,96,128]{2,0,1:T(4,128)} %copy.16), calls=%async_computation.1 | async-start | bytes 393216 | tf_op jit(solution)/shard_map/all_to_all | solution.py:111
  10.6 3.9 %collective-permute-start.1 = (f32[4,1,8,128]{3,2,1,0:T(8,128)S(1)}, f32[4,1,8,128]{3,2,1,0:T(8,128)S(1)}, u32[]{:S(2)}, u32[]{:S(2)}) collective-permute-start(f32[4,1,8,128]{3,2,1,0:T(8,128)S(1)} %get-tuple-element.156), channel_id=1, source_target_pairs={{0,4},{4,8},{8,12},{1,5},{5,9},{9,13},{2,6},{6,10},{10,14},{3,7},{... | collective-permute-start | bytes 49160 | tf_op jit(solution)/shard_map/ppermute | solution.py:16
  14.5 1.3 %collective-permute-start = (f32[4,1,8,128]{3,2,1,0:T(8,128)S(1)}, f32[4,1,8,128]{3,2,1,0:T(8,128)S(1)}, u32[]{:S(2)}, u32[]{:S(2)}) collective-permute-start(f32[4,1,8,128]{3,2,1,0:T(8,128)S(1)} %get-tuple-element.155), channel_id=1, source_target_pairs={{4,0},{8,4},{12,8},{5,1},{9,5},{13,9},{6,2},{10,6},{14,10},{7,3},{... | collective-permute-start | bytes 49160 | tf_op jit(solution)/shard_map/ppermute | solution.py:19
  17.0 3.1 %collective-permute-done = f32[4,1,8,128]{3,2,1,0:T(8,128)S(1)} collective-permute-done((f32[4,1,8,128]{3,2,1,0:T(8,128)S(1)}, f32[4,1,8,128]{3,2,1,0:T(8,128)S(1)}, u32[]{:S(2)}, u32[]{:S(2)}) %collective-permute-start) | collective-permute-done | bytes 16416 | tf_op jit(solution)/shard_map/ppermute | solution.py:19
  20.2 1.3 %collective-permute-start.2 = (f32[4,6,1,128]{3,2,1,0:T(1,128)S(1)}, f32[4,6,1,128]{3,2,1,0:T(1,128)S(1)}, u32[]{:S(2)}, u32[]{:S(2)}) collective-permute-start(f32[4,6,1,128]{3,2,1,0:T(1,128)S(1)} %get-tuple-element.154), channel_id=1, source_target_pairs={{2,0},{3,1},{6,4},{7,5},{10,8},{11,9},{14,12},{15,13},{18,16},{19,... | collective-permute-start | bytes 36872 | tf_op jit(solution)/shard_map/ppermute | solution.py:19
  21.5 4.5 %collective-permute-start.3 = (f32[4,6,1,128]{3,2,1,0:T(1,128)S(1)}, f32[4,6,1,128]{3,2,1,0:T(1,128)S(1)}, u32[]{:S(2)}, u32[]{:S(2)}) collective-permute-start(f32[4,6,1,128]{3,2,1,0:T(1,128)S(1)} %get-tuple-element.153), channel_id=1, source_target_pairs={{0,2},{1,3},{4,6},{5,7},{8,10},{9,11},{12,14},{13,15},{16,18},{17,... | collective-permute-start | bytes 36872 | tf_op jit(solution)/shard_map/ppermute | solution.py:16
  26.0 3.6 %all-to-all-start = ((f32[4,96,128]{2,0,1:T(4,128)}), f32[4,96,128]{2,0,1:T(4,128)S(1)}, u32[]{:S(2)}, u32[]{:S(2)}) async-start(f32[4,96,128]{2,0,1:T(4,128)} %copy.15), calls=%async_computation | async-start | bytes 393216 | tf_op jit(solution)/shard_map/all_to_all | solution.py:110
  30.9 5.0 %all-to-all-done = f32[4,96,128]{2,0,1:T(4,128)S(1)} async-done(((f32[4,96,128]{2,0,1:T(4,128)}), f32[4,96,128]{2,0,1:T(4,128)S(1)}, u32[]{:S(2)}, u32[]{:S(2)}) %all-to-all-start) | async-done | bytes 196640 | tf_op jit(solution)/shard_map/all_to_all | solution.py:110
  35.9 3.3 %all-to-all-start.2 = ((s32[1,96,128]{2,0,1:T(1,128)}), s32[1,96,128]{2,0,1:T(1,128)S(1)}, u32[]{:S(2)}, u32[]{:S(2)}) async-start(s32[1,96,128]{2,0,1:T(1,128)} %bitcast.14), calls=%async_computation.2 | async-start | bytes 98304 | tf_op jit(solution)/shard_map/all_to_all | solution.py:112
  39.4 5.5 %all-to-all-done.2 = s32[1,96,128]{2,0,1:T(1,128)S(1)} async-done(((s32[1,96,128]{2,0,1:T(1,128)}), s32[1,96,128]{2,0,1:T(1,128)S(1)}, u32[]{:S(2)}, u32[]{:S(2)}) %all-to-all-start.2) | async-done | bytes 49184 | tf_op jit(solution)/shard_map/all_to_all | solution.py:112
  44.9 31.3 %while.26 = (s32[]{:T(128)}, f32[8,32,128]{2,1,0:T(8,128)S(1)}, f32[24,8,4,128]{3,2,1,0:T(4,128)S(1)}, s32[24,4,128]{2,1,0:T(4,128)S(1)}, s32[]{:T(128)}, /*index=5*/s32[]{:T(128)}) while((s32[]{:T(128)}, f32[8,32,128]{2,1,0:T(8,128)S(1)}, f32[24,8,4,128]{3,2,1,0:T(4,128)S(1)}, s32[24,4,128]{2,1,0:T(4,128)S(1)}, s32[]{:T(128)}, ...), condition=%wide.region_2.3_spmd.clone, body=%wide.region_1.2_spmd.clone.sunk | while | flops 202073600 | bytes 845919 | solution.py:62
  46.4 1.1 fusion.66
  47.7 1.1 fusion.66
  50.3 1.1 fusion.66
  51.6 1.1 fusion.66
  52.9 1.1 fusion.66
  54.2 1.1 fusion.66
  56.8 1.1 fusion.66
  58.1 1.1 fusion.66
  59.4 1.1 fusion.66
  60.7 1.1 fusion.66
  63.3 1.1 fusion.66
  64.6 1.1 fusion.66
  65.9 1.1 fusion.66
  67.2 1.1 fusion.66
  69.8 1.1 fusion.66
  71.1 1.1 fusion.66
  73.7 1.1 fusion.66
  76.3 31.9 %while.25 = (s32[]{:T(128)}, f32[24,4,4,128]{3,2,1,0:T(4,128)}, s32[24,4,128]{2,1,0:T(4,128)S(1)}, f32[4,32,128]{2,1,0:T(8,128)S(1)}, s32[]{:T(128)}) while((s32[]{:T(128)}, f32[24,4,4,128]{3,2,1,0:T(4,128)}, s32[24,4,128]{2,1,0:T(4,128)S(1)}, f32[4,32,128]{2,1,0:T(8,128)S(1)}, s32[]{:T(128)}) %tuple.72), condition=%wide.region_5.6_spmd, body=%wide.region_3.5_spmd.sunk | while | flops 101342720 | bytes 624717 | solution.py:81
  108.2 3.4 %all-to-all-start.3 = ((f32[4,96,128]{2,0,1:T(4,128)}), f32[4,96,128]{2,0,1:T(4,128)S(1)}, u32[]{:S(2)}, u32[]{:S(2)}) async-start(f32[4,96,128]{2,0,1:T(4,128)} %bitcast.20), calls=%async_computation.3 | async-start | bytes 393216 | tf_op jit(solution)/shard_map/all_to_all | solution.py:130
  112.2 5.6 %all-to-all-done.3 = f32[4,96,128]{2,0,1:T(4,128)S(1)} async-done(((f32[4,96,128]{2,0,1:T(4,128)}), f32[4,96,128]{2,0,1:T(4,128)S(1)}, u32[]{:S(2)}, u32[]{:S(2)}) %all-to-all-start.3) | async-done | bytes 196640 | tf_op jit(solution)/shard_map/all_to_all | solution.py:130
  (207 shorter events, 49.7 us)
Async XLA Ops:
  3.4 7.2 %copy-start = (f32[4,4,8,128]{3,2,1,0:T(8,128)S(1)}, f32[4,4,8,128]{3,2,1,0:T(8,128)}, u32[]{:S(2)}) copy-start(f32[4,4,8,128]{3,2,1,0:T(8,128)} %param.10) | copy-start | bytes 196612
  3.4 12.4 %copy-start.1 = (f32[4,4096]{1,0:T(4,128)S(1)}, f32[4,4096]{1,0:T(4,128)}, u32[]{:S(2)}) copy-start(f32[4,4096]{1,0:T(4,128)} %param.12) | copy-start | bytes 196612
  4.2 21.8 %all-to-all-start.1 = ((f32[4,96,128]{2,0,1:T(4,128)}), f32[4,96,128]{2,0,1:T(4,128)S(1)}, u32[]{:S(2)}, u32[]{:S(2)}) async-start(f32[4,96,128]{2,0,1:T(4,128)} %copy.16), calls=%async_computation.1 | async-start | bytes 393216 | tf_op jit(solution)/shard_map/all_to_all | solution.py:111
  10.6 6.4 %collective-permute-start.1 = (f32[4,1,8,128]{3,2,1,0:T(8,128)S(1)}, f32[4,1,8,128]{3,2,1,0:T(8,128)S(1)}, u32[]{:S(2)}, u32[]{:S(2)}) collective-permute-start(f32[4,1,8,128]{3,2,1,0:T(8,128)S(1)} %get-tuple-element.156), channel_id=1, source_target_pairs={{0,4},{4,8},{8,12},{1,5},{5,9},{9,13},{2,6},{6,10},{10,14},{3,7},{... | collective-permute-start | bytes 49160 | tf_op jit(solution)/shard_map/ppermute | solution.py:16
  14.5 5.6 %collective-permute-start = (f32[4,1,8,128]{3,2,1,0:T(8,128)S(1)}, f32[4,1,8,128]{3,2,1,0:T(8,128)S(1)}, u32[]{:S(2)}, u32[]{:S(2)}) collective-permute-start(f32[4,1,8,128]{3,2,1,0:T(8,128)S(1)} %get-tuple-element.155), channel_id=1, source_target_pairs={{4,0},{8,4},{12,8},{5,1},{9,5},{13,9},{6,2},{10,6},{14,10},{7,3},{... | collective-permute-start | bytes 49160 | tf_op jit(solution)/shard_map/ppermute | solution.py:19
  17.0 12.7 %copy-start.2 = (s32[4096]{0:T(1024)S(1)}, s32[4096]{0:T(1024)}, u32[]{:S(2)}) copy-start(s32[4096]{0:T(1024)} %param.14) | copy-start | bytes 49156
  20.2 10.4 %collective-permute-start.2 = (f32[4,6,1,128]{3,2,1,0:T(1,128)S(1)}, f32[4,6,1,128]{3,2,1,0:T(1,128)S(1)}, u32[]{:S(2)}, u32[]{:S(2)}) collective-permute-start(f32[4,6,1,128]{3,2,1,0:T(1,128)S(1)} %get-tuple-element.154), channel_id=1, source_target_pairs={{2,0},{3,1},{6,4},{7,5},{10,8},{11,9},{14,12},{15,13},{18,16},{19,... | collective-permute-start | bytes 36872 | tf_op jit(solution)/shard_map/ppermute | solution.py:19
  21.5 9.1 %collective-permute-start.3 = (f32[4,6,1,128]{3,2,1,0:T(1,128)S(1)}, f32[4,6,1,128]{3,2,1,0:T(1,128)S(1)}, u32[]{:S(2)}, u32[]{:S(2)}) collective-permute-start(f32[4,6,1,128]{3,2,1,0:T(1,128)S(1)} %get-tuple-element.153), channel_id=1, source_target_pairs={{0,2},{1,3},{4,6},{5,7},{8,10},{9,11},{12,14},{13,15},{16,18},{17,... | collective-permute-start | bytes 36872 | tf_op jit(solution)/shard_map/ppermute | solution.py:16
  26.0 9.9 %all-to-all-start = ((f32[4,96,128]{2,0,1:T(4,128)}), f32[4,96,128]{2,0,1:T(4,128)S(1)}, u32[]{:S(2)}, u32[]{:S(2)}) async-start(f32[4,96,128]{2,0,1:T(4,128)} %copy.15), calls=%async_computation | async-start | bytes 393216 | tf_op jit(solution)/shard_map/all_to_all | solution.py:110
  35.9 8.9 %all-to-all-start.2 = ((s32[1,96,128]{2,0,1:T(1,128)}), s32[1,96,128]{2,0,1:T(1,128)S(1)}, u32[]{:S(2)}, u32[]{:S(2)}) async-start(s32[1,96,128]{2,0,1:T(1,128)} %bitcast.14), calls=%async_computation.2 | async-start | bytes 98304 | tf_op jit(solution)/shard_map/all_to_all | solution.py:112
  44.9 31.3 %copy-start.3 = (f32[4]{0:T(128)S(1)}, f32[4]{0:T(128)}, u32[]{:S(2)}) copy-start(f32[4]{0:T(128)} %param.11) | copy-start | bytes 52
  108.2 9.6 %all-to-all-start.3 = ((f32[4,96,128]{2,0,1:T(4,128)}), f32[4,96,128]{2,0,1:T(4,128)S(1)}, u32[]{:S(2)}, u32[]{:S(2)}) async-start(f32[4,96,128]{2,0,1:T(4,128)} %bitcast.20), calls=%async_computation.3 | async-start | bytes 393216 | tf_op jit(solution)/shard_map/all_to_all | solution.py:130
where the time goes:
time: 119 us
  matrix products  45.3 us (38%)
  starting transfers between devices  27.7 us (23%)
  waiting for transfers between devices  19.2 us (16%)
  local copies, waits for them, and re-layouts  17.1 us (14%)
  other arithmetic  7.06 us (6%)
  loops' own time  1.48 us (1%)
    dot_general x24, matrix products, step(): part = jnp.einsum('gch,qgcl->gqhl', onehot_high, weighted, precision=HIGH)  26.3 us
    dot_general x24, matrix products, step(): picked = jnp.einsum('gch,shl->gscl', onehot_high, table, precision=HIGH)  16.3 us
    dynamic_update_slice x24, local copies, waits for them, and re-layouts, block_reads(): lax.scan(step, 0, (grouped_vox, jnp.arange(steps_count, dtype=jnp.int32)))  14.4 us
    ppermute x2, starting transfers between devices, extended(): lax.ppermute(lax.slice_in_dim(block, block.shape[dim] - width, None, axis...  8.46 us
    all_to_all x1, starting transfers between devices, deposit(): lax.all_to_all(send_uptake, 'gz', split_axis=1, concat_axis=1, tiled=True)  6.35 us
    all_to_all x1, waiting for transfers between devices, reader(): lax.all_to_all(looked_up, 'gz', split_axis=1, concat_axis=1, tiled=True)  5.57 us
    all_to_all x1, waiting for transfers between devices, deposit(): lax.all_to_all(send_index, 'gz', split_axis=1, concat_axis=1, tiled=True)  5.47 us
    all_to_all x1, waiting for transfers between devices, deposit(): lax.all_to_all(send_release, 'gz', split_axis=1, concat_axis=1, tiled=True)  5.03 us
  transfers between devices with their start and end apart: 8, of which 4 were waited for; matrix products, arithmetic and copies ran while one was open for 3% of the time, Pallas kernels for 0%

commit v1 on v0

v1 whole, which is shorter than its diff:
```python
import functools

import jax
import jax.numpy as jnp
from jax import lax
from jax.experimental import pallas as pl
from jax.experimental.pallas import tpu as pltpu
from jax.sharding import PartitionSpec as P

MESH = pl.DeviceIdType.MESH
F32 = jnp.float32
BF16 = jnp.bfloat16


def split(x):
    high = x.astype(BF16).astype(F32)
    return high, x - high


def kernel(
    n, ny, chunk,
    field, diffusion, secrete, uptake, index,
    updated, conc,
    sec_buf, upt_buf, idx_buf, table, z_low, z_high, y_low, y_high, acc, own_low,
    send_sem, recv_sem, halo_send, halo_recv, tab_send, tab_recv,
):
    z = lax.axis_index("gz")
    y = lax.axis_index("gy")
    subs, planes, rows, lanes = field.shape
    cells = secrete.shape[1]
    width = 2 * lanes
    shift = width.bit_length() - 1
    half = planes * rows // 2
    half_planes = planes // 2
    barrier = pltpu.get_barrier_semaphore()
    sides = (
        (z > 0, {"gz": z - 1}),
        (z < n - 1, {"gz": z + 1}),
        (y > 0, {"gy": y - 1}),
        (y < ny - 1, {"gy": y + 1}),
    )
    for there, device in sides:
        @pl.when(there)
        def _():
            pl.semaphore_signal(barrier, inc=1, device_id=device, device_id_type=MESH)
    pl.semaphore_wait(barrier, sum(jnp.where(there, 1, 0) for there, unused in sides))

    bufs = (idx_buf, sec_buf, upt_buf)
    owns = (index, secrete, uptake)

    def remote(src, dst, send, recv, device):
        return pltpu.make_async_remote_copy(
            src_ref=src, dst_ref=dst, send_sem=send, recv_sem=recv,
            device_id=device, device_id_type=MESH,
        )

    def cell_copy(arr, way, step, slot, src):
        return remote(
            src, bufs[arr].at[slot], send_sem.at[way, step, arr], recv_sem.at[slot, arr],
            sides[way][1],
        )

    def table_copy(way, step, slot, src):
        return remote(
            src, table.at[slot], tab_send.at[way, step], tab_recv.at[slot], sides[way][1]
        )

    halo = (
        remote(field.at[:, 0], z_high, halo_send.at[0], halo_recv.at[0], sides[0][1]),
        remote(field.at[:, planes - 1], z_low, halo_send.at[1], halo_recv.at[1], sides[1][1]),
        remote(field, y_high, halo_send.at[2], halo_recv.at[2], sides[2][1]),
        remote(field, y_low, halo_send.at[3], halo_recv.at[3], sides[3][1]),
    )
    from_side = (1, 0, 3, 2)

    for arr in range(3):
        for way in range(2):
            @pl.when(sides[way][0])
            def _():
                cell_copy(arr, way, 0, z, owns[arr]).start()
    for way in range(4):
        @pl.when(sides[way][0])
        def _():
            halo[way].start()

    acc[...] = jnp.zeros_like(acc)

    def keys(word):
        return lax.shift_right_logical(word, shift), word & (width - 1)

    def deposit(idx, sec, upt, save):
        def step(k, carry):
            at = pl.ds(pl.multiple_of(k * chunk, chunk), chunk)
            key, low = keys(idx[:, at])
            mask = lax.broadcasted_iota(jnp.int32, (half, chunk), 0) == key - half * z
            low_hot = (lax.broadcasted_iota(jnp.int32, (width, chunk), 0) == low).astype(F32)
            low_hot = low_hot.astype(BF16)
            if save:
                own_low[:, at] = low_hot
            parts = split(sec[:, at]) + split(upt[:, at])
            weighted = []
            for part in parts:
                for s in range(subs):
                    row = jnp.broadcast_to(part[s : s + 1], (half, chunk))
                    weighted.append(jnp.where(mask, row, 0.0).astype(BF16))
            weighted = jnp.concatenate(weighted, axis=0)
            acc[...] += lax.dot_general(
                weighted, low_hot, (((1,), (1,)), ((), ())), preferred_element_type=F32
            )
            return carry

        lax.fori_loop(0, cells // chunk, step, 0)

    deposit(index, secrete, uptake, True)

    def gather_step(t, carry):
        slots = (z + t, z - t)
        arrived = (z + t < n, z - t >= 0)
        for arr in range(3):
            for way in range(2):
                slot = slots[way]

                @pl.when(arrived[way])
                def _():
                    remote(
                        bufs[arr].at[slot], bufs[arr].at[slot], send_sem.at[way, t, arr],
                        recv_sem.at[slot, arr], sides[1 - way][1],
                    ).wait_recv()

                    @pl.when(sides[way][0])
                    def _():
                        cell_copy(arr, way, t, slot, bufs[arr].at[slot]).start()
        for way in range(2):
            slot = slots[way]

            @pl.when(arrived[way])
            def _():
                deposit(idx_buf.at[slot], sec_buf.at[slot], upt_buf.at[slot], False)

        return carry

    lax.fori_loop(1, n, gather_step, 0)

    for way in range(4):
        @pl.when(sides[way][0])
        def _():
            halo[from_side[way]].wait_recv()

    lane = lax.broadcasted_iota(jnp.int32, (rows, lanes), 1)
    line = lax.broadcasted_iota(jnp.int32, (rows, lanes), 0)
    has_z = ((z > 0), (z < n - 1))
    has_y = ((y > 0), (y < ny - 1))
    for s in range(subs):
        rate = diffusion[s]
        for p in range(planes):
            here = field[s, p]
            if p > 0:
                below = field[s, p - 1]
            else:
                below = jnp.where(has_z[0], z_low[s], 0.0)
            if p < planes - 1:
                above = field[s, p + 1]
            else:
                above = jnp.where(has_z[1], z_high[s], 0.0)
            edge_low = jnp.where(has_y[0], y_low[s, p], 0.0)
            edge_high = jnp.where(has_y[1], y_high[s, p], 0.0)
            prev = jnp.where(
                line == 0, pltpu.roll(edge_low, 1, 0), pltpu.roll(here, 1, 0)
            )
            following = jnp.where(
                line == rows - 1,
                pltpu.roll(edge_high, rows - 1, 0),
                pltpu.roll(here, rows - 1, 0),
            )
            left = jnp.where(lane == 0, 0.0, pltpu.roll(here, 1, 1))
            right = jnp.where(lane == lanes - 1, 0.0, pltpu.roll(here, lanes - 1, 1))
            total = above + below + following + prev + right + left
            diffused = here + rate * (total - 6.0 * here)
            col = pl.ds((p // half_planes) * lanes, lanes)
            row = (p % half_planes) * rows

            def summed(part):
                first = acc[pl.ds((part * subs + s) * half + row, rows), col]
                return first + acc[pl.ds(((part + 1) * subs + s) * half + row, rows), col]

            updated[s, p] = (diffused + summed(0)) / (1.0 + summed(2))

    for way in range(2):
        @pl.when(sides[way][0])
        def _():
            table_copy(way, 0, z, updated).start()

    def look_up(tab, slot, first):
        left = [tab[:, p].reshape(subs, rows, lanes) for p in range(planes)]
        low_half = jnp.concatenate(left[:half_planes], axis=1)
        high_half = jnp.concatenate(left[half_planes:], axis=1)
        values = jnp.concatenate([low_half, high_half], axis=2).reshape(subs * half, width)
        high_part, low_part = split(values)
        both = jnp.concatenate([high_part, low_part], axis=0).astype(BF16)

        def step(k, carry):
            at = pl.ds(pl.multiple_of(k * chunk, chunk), chunk)
            key, unused = keys(index[:, at])
            mask = lax.broadcasted_iota(jnp.int32, (half, chunk), 0) == key - half * slot
            picked = jnp.dot(both, own_low[:, at], preferred_element_type=F32)
            picked = picked[: subs * half] + picked[subs * half :]
            for s in range(subs):
                part = jnp.where(mask, picked[s * half : (s + 1) * half], 0.0)
                part = jnp.sum(part, axis=0, keepdims=True)
                if first:
                    conc[s : s + 1, at] = part
                else:
                    conc[s : s + 1, at] += part
            return carry

        lax.fori_loop(0, cells // chunk, step, 0)

    look_up(updated, z, True)

    def return_step(t, carry):
        slots = (z + t, z - t)
        arrived = (z + t < n, z - t >= 0)
        for way in range(2):
            slot = slots[way]

            @pl.when(arrived[way])
            def _():
                remote(
                    table.at[slot], table.at[slot], tab_send.at[way, t], tab_recv.at[slot],
                    sides[1 - way][1],
                ).wait_recv()

                @pl.when(sides[way][0])
                def _():
                    table_copy(way, t, slot, table.at[slot]).start()

        for way in range(2):
            slot = slots[way]

            @pl.when(arrived[way])
            def _():
                look_up(table.at[slot], slot, False)

        return carry

    lax.fori_loop(1, n, return_step, 0)

    for way in range(4):
        @pl.when(sides[way][0])
        def _():
            halo[way].wait_send()

    def drain(t, carry):
        slots = (z + t, z - t)
        sent = (z + t < n, z - t >= 0)
        for way in range(2):
            @pl.when(sent[way] & sides[way][0])
            def _():
                for arr in range(3):
                    cell_copy(arr, way, t, slots[way], bufs[arr].at[slots[way]]).wait_send()
                table_copy(way, t, slots[way], table.at[slots[way]]).wait_send()

        return carry

    lax.fori_loop(0, n, drain, 0)


def shards(n, ny, field, diffusion, secrete, uptake, cell_voxel, block_dest):
    subs, planes, rows, lanes = field.shape
    cells = secrete.shape[1]
    blocks = block_dest.shape[0]
    half = planes * rows // 2
    width = 2 * lanes
    assert planes % 2 == 0 and width & (width - 1) == 0
    voxel = cell_voxel.reshape(blocks, cells // blocks)
    line = voxel // lanes
    key = line % half + half * block_dest
    index = (key * width + voxel % lanes + lanes * (line // half)).reshape(1, cells)
    chunk = 512
    dma = pltpu.SemaphoreType.DMA
    vmem = pl.BlockSpec(memory_space=pltpu.VMEM)
    return pl.pallas_call(
        functools.partial(kernel, n, ny, chunk),
        out_shape=(
            jax.ShapeDtypeStruct(field.shape, F32),
            jax.ShapeDtypeStruct(secrete.shape, F32),
        ),
        in_specs=[vmem, pl.BlockSpec(memory_space=pltpu.SMEM), vmem, vmem, vmem],
        out_specs=(vmem, vmem),
        scratch_shapes=[
            pltpu.VMEM((n, subs, cells), F32),
            pltpu.VMEM((n, subs, cells), F32),
            pltpu.VMEM((n, 1, cells), jnp.int32),
            pltpu.VMEM((n,) + field.shape, F32),
            pltpu.VMEM((subs, rows, lanes), F32),
            pltpu.VMEM((subs, rows, lanes), F32),
            pltpu.VMEM(field.shape, F32),
            pltpu.VMEM(field.shape, F32),
            pltpu.VMEM((4 * subs * half, width), F32),
            pltpu.VMEM((width, cells), BF16),
            dma((2, n, 3)),
            dma((n, 3)),
            dma((4,)),
            dma((4,)),
            dma((2, n)),
            dma((n,)),
        ],
        compiler_params=pltpu.CompilerParams(collective_id=0, has_side_effects=True),
    )(field, diffusion, secrete, uptake, index)


def solution(mesh):
    in_specs = (
        P("sa", ("grp", "gz"), "gy", None),
        P("sa"),
        P("sa", ("grp", "gz", "gy")),
        P("sa", ("grp", "gz", "gy")),
        P(("grp", "gz", "gy")),
        P(("grp", "gz", "gy"), None),
    )
    out_specs = (P("sa", ("grp", "gz"), "gy", None), P("sa", ("grp", "gz", "gy")))
    return jax.shard_map(
        functools.partial(shards, mesh.shape["gz"], mesh.shape["gy"]),
        mesh=mesh, in_specs=in_specs, out_specs=out_specs, check_vma=False,
    )
```

time: 119 us -> 39.7 us (0.33)
  matrix products: 45.3 us -> 0 us
  Pallas kernels: 0 us -> 34.5 us
  starting transfers between devices: 27.7 us -> 0 us
  waiting for transfers between devices: 19.2 us -> 0 us
  local copies, waits for them, and re-layouts: 17.1 us -> 2.14 us
  other arithmetic: 7.06 us -> 2.05 us
  loops' own time: 1.48 us -> 0 us
    dot_general x52 -> x0, matrix products: 45.3 us -> none  [the longest x24 26.3 us: step(): part = jnp.einsum('gch,qgcl->gqhl', onehot_high, weighted, precision=HIGH)]
    pallas_call x0 -> x1, Pallas kernels: none -> 34.5 us  [shards(): pl.pallas_call(functools.partial(kernel, n, ny, chunk), out_shape=(jax.Sh...]
    all_to_all x4 -> x0, starting transfers between devices: 16.6 us -> none  [the longest x1 6.35 us: deposit(): lax.all_to_all(send_uptake, 'gz', split_axis=1, concat_axis=1, tiled=True)]
    all_to_all x4 -> x0, waiting for transfers between devices: 16.1 us -> none  [the longest x1 5.57 us: reader(): lax.all_to_all(looked_up, 'gz', split_axis=1, concat_axis=1, tiled=True)]
    dynamic_update_slice x24 -> x0, local copies, waits for them, and re-layouts: 14.4 us -> none  [block_reads(): lax.scan(step, 0, (grouped_vox, jnp.arange(steps_count, dtype=jnp.int32)))]
    ppermute x4 -> x0, starting transfers between devices: 11 us -> none  [the longest x2 8.46 us: extended(): lax.ppermute(lax.slice_in_dim(block, block.shape[dim] - width, None, axis...]
    convert_element_type x48 -> x0, other arithmetic: 3.76 us -> none  [one_hots(): ((voxel_group % lanes)[..., None] == lane_ids).astype(jnp.float32)]
    ppermute x4 -> x0, waiting for transfers between devices: 3.14 us -> none  [the longest x2 3.13 us: extended(): lax.ppermute(lax.slice_in_dim(block, 0, width, axis=dim), axis, backward)]
  transfers between devices with their start and end apart: 8 -> 0, of which waited for: 4 -> 0; matrix products, arithmetic and copies ran while one was open for 3% -> 0% of each run, Pallas kernels for 0% -> 0%
where the time goes in v1:
time: 39.7 us; the launch traced here: 39.4 us
  Pallas kernels  34.5 us (87%)
  local copies, waits for them, and re-layouts  2.14 us (5%)
  other arithmetic  2.05 us (5%)
  between operations  0.65 us (2%)
    pallas_call x1, Pallas kernels, shards(): pl.pallas_call(functools.partial(kernel, n, ny, chunk), out_shape=(jax.Sh...  34.5 us
    unnamed x4, local copies, waits for them, and re-layouts  2.14 us
    add x1, other arithmetic, shards(): key * width + voxel % lanes + lanes * (line // half)  1.4 us

profile of v1, /device:TPU:0, one launch (start us, length us, event | category | flops | bytes accessed | tf_op | source)
XLA Modules:
  0.0 39.4 jit_solution(12228677013690079664)
XLA Ops:
  0.6 0.7 %multiply_bitcast_fusion = s32[32]{0:T(128)S(1)} fusion(s32[32,1]{0,1:T(1,128)} %param.11), kind=kLoop, calls=%fused_computation.23 | loop fusion | flops 32 | bytes 256 | tf_op jit(solution)/shard_map/add | solution.py:277
  1.3 1.4 %fusion.3 = s32[4096]{0:T(1024)} fusion(s32[4096]{0:T(1024)} %param.10, s32[32]{0:T(128)S(1)} %multiply_bitcast_fusion), kind=kLoop, calls=%fused_computation.13 | loop fusion | flops 176128 | bytes 32896 | tf_op jit(solution)/shard_map/add | solution.py:278
  2.7 34.5 %shard_map.77 = (f32[4,4,8,128]{3,2,1,0:T(8,128)}, f32[4,4096]{1,0:T(4,128)}) custom-call(f32[4,4,8,128]{3,2,1,0:T(8,128)} %field.1, f32[4]{0:T(128)} %diffusion.1, f32[4,4096]{1,0:T(4,128)} %secrete.1, f32[4,4096]{1,0:T(4,128)} %uptake.1, s32[1,4096]{1,0:T(1,128)} %bitcast.5), custom_call_target="tpu_custom_call" | custom-call | tf_op jit(solution)/shard_map/pallas_call | solution.py:282
  37.2 0.0 copy-start
  37.2 1.5 %copy.10 = f32[4,4,8,128]{3,2,1,0:T(8,128)} copy(f32[4,4,8,128]{3,2,1,0:T(8,128)} %get-tuple-element.4) | data formatting | bytes 131072
  38.8 0.0 copy-done
  38.8 0.6 %copy.11 = f32[4,4096]{1,0:T(4,128)} copy(f32[4,4096]{1,0:T(4,128)S(1)} %copy-done) | data formatting | bytes 131072
Async XLA Ops:
  37.2 1.5 %copy-start = (f32[4,4096]{1,0:T(4,128)S(1)}, f32[4,4096]{1,0:T(4,128)}, u32[]{:S(2)}) copy-start(f32[4,4096]{1,0:T(4,128)} %get-tuple-element.5) | copy-start | bytes 196612

commit v2 on v1

--- a/solution.py
+++ b/solution.py
@@ -18,11 +18,11 @@
 
 
 def kernel(
-    n, ny, chunk,
-    field, diffusion, secrete, uptake, index,
+    n, ny, chunk, pieces,
+    field_in, diffusion, secrete, uptake, voxel_in, targets,
     updated, conc,
-    sec_buf, upt_buf, idx_buf, table, z_low, z_high, y_low, y_high, acc, own_low,
-    send_sem, recv_sem, halo_send, halo_recv, tab_send, tab_recv,
+    field, voxel, sec_buf, upt_buf, idx_buf, table, z_low, z_high, y_low, y_high, acc, own_low,
+    local_sem, send_sem, recv_sem, halo_send, halo_recv, tab_send, tab_recv,
 ):
     z = lax.axis_index("gz")
     y = lax.axis_index("gy")
@@ -32,6 +32,17 @@
     shift = width.bit_length() - 1
     half = planes * rows // 2
     half_planes = planes // 2
+    blocks = targets.shape[0]
+    per_block = cells // blocks
+    area = planes * rows
+    loads = (
+        pltpu.make_async_copy(voxel_in, voxel, local_sem.at[0]),
+        pltpu.make_async_copy(secrete, sec_buf.at[z], local_sem.at[1]),
+        pltpu.make_async_copy(uptake, upt_buf.at[z], local_sem.at[2]),
+        pltpu.make_async_copy(field_in, field, local_sem.at[3]),
+    )
+    for load in loads:
+        load.start()
     barrier = pltpu.get_barrier_semaphore()
     sides = (
         (z > 0, {"gz": z - 1}),
@@ -43,10 +54,32 @@
         @pl.when(there)
         def _():
             pl.semaphore_signal(barrier, inc=1, device_id=device, device_id_type=MESH)
+    acc[...] = jnp.zeros_like(acc)
+    loads[0].wait()
+    for b in range(blocks):
+        at = pl.ds(b * per_block, per_block)
+        own = voxel[:, at]
+        line_id = lax.shift_right_logical(own, shift - 1)
+        side = jnp.where(line_id >= half, 1, 0)
+        key = line_id - half * side + half * targets[b]
+        idx_buf[z, :, at] = key * width + (own & (lanes - 1)) + lanes * side
+    for load in loads[1:]:
+        load.wait()
     pl.semaphore_wait(barrier, sum(jnp.where(there, 1, 0) for there, unused in sides))
 
-    bufs = (idx_buf, sec_buf, upt_buf)
-    owns = (index, secrete, uptake)
+    part = cells // 2
+    spans = (
+        (sec_buf, 0, part), (sec_buf, part, part), (idx_buf, 0, cells),
+        (upt_buf, 0, part), (upt_buf, part, part),
+    )
+    depth = subs * area // pieces
+
+    def cell_ref(arr, slot):
+        buf, first, size = spans[arr]
+        return buf.at[slot, :, pl.ds(first, size)]
+
+    def table_ref(piece, slot):
+        return table.at[slot, pl.ds(piece * depth, depth)]
 
     def remote(src, dst, send, recv, device):
         return pltpu.make_async_remote_copy(
@@ -54,15 +87,18 @@
             device_id=device, device_id_type=MESH,
         )
 
-    def cell_copy(arr, way, step, slot, src):
+    def cell_copy(arr, way, step, slot, side):
+        ref = cell_ref(arr, slot)
         return remote(
-            src, bufs[arr].at[slot], send_sem.at[way, step, arr], recv_sem.at[slot, arr],
-            sides[way][1],
+            ref, ref, send_sem.at[way, step, arr], recv_sem.at[slot, arr], sides[side][1]
         )
 
-    def table_copy(way, step, slot, src):
+    def table_copy(piece, way, step, slot, side):
+        ref = table_ref(piece, slot)
+        src = updated.at[pl.ds(piece * depth, depth)] if step is None else ref
         return remote(
-            src, table.at[slot], tab_send.at[way, step], tab_recv.at[slot], sides[way][1]
+            src, ref, tab_send.at[way, 0 if step is None else step, piece],
+            tab_recv.at[slot, piece], sides[side][1],
         )
 
     halo = (
@@ -73,17 +109,15 @@
     )
     from_side = (1, 0, 3, 2)
 
-    for arr in range(3):
+    for arr in range(len(spans)):
         for way in range(2):
             @pl.when(sides[way][0])
             def _():
-                cell_copy(arr, way, 0, z, owns[arr]).start()
+                cell_copy(arr, way, 0, z, way).start()
     for way in range(4):
         @pl.when(sides[way][0])
         def _():
             halo[way].start()
-
-    acc[...] = jnp.zeros_like(acc)
 
     def keys(word):
         return lax.shift_right_logical(word, shift), word & (width - 1)
@@ -111,25 +145,22 @@
 
         lax.fori_loop(0, cells // chunk, step, 0)
 
-    deposit(index, secrete, uptake, True)
+    deposit(idx_buf.at[z], sec_buf.at[z], upt_buf.at[z], True)
 
     def gather_step(t, carry):
         slots = (z + t, z - t)
         arrived = (z + t < n, z - t >= 0)
-        for arr in range(3):
+        for arr in range(len(spans)):
             for way in range(2):
                 slot = slots[way]
 
                 @pl.when(arrived[way])
                 def _():
-                    remote(
-                        bufs[arr].at[slot], bufs[arr].at[slot], send_sem.at[way, t, arr],
-                        recv_sem.at[slot, arr], sides[1 - way][1],
-                    ).wait_recv()
+                    cell_copy(arr, way, t, slot, 1 - way).wait_recv()
 
                     @pl.when(sides[way][0])
                     def _():
-                        cell_copy(arr, way, t, slot, bufs[arr].at[slot]).start()
+                        cell_copy(arr, way, t, slot, way).start()
         for way in range(2):
             slot = slots[way]
 
@@ -183,24 +214,24 @@
                 first = acc[pl.ds((part * subs + s) * half + row, rows), col]
                 return first + acc[pl.ds(((part + 1) * subs + s) * half + row, rows), col]
 
-            updated[s, p] = (diffused + summed(0)) / (1.0 + summed(2))
+            updated[pl.ds((s * planes + p) * rows, rows)] = (diffused + summed(0)) / (1.0 + summed(2))
 
     for way in range(2):
         @pl.when(sides[way][0])
         def _():
-            table_copy(way, 0, z, updated).start()
+            for piece in range(pieces):
+                table_copy(piece, way, None, z, way).start()
 
     def look_up(tab, slot, first):
-        left = [tab[:, p].reshape(subs, rows, lanes) for p in range(planes)]
-        low_half = jnp.concatenate(left[:half_planes], axis=1)
-        high_half = jnp.concatenate(left[half_planes:], axis=1)
-        values = jnp.concatenate([low_half, high_half], axis=2).reshape(subs * half, width)
+        values = tab[...].reshape(subs, 2, half, lanes)
+        values = jnp.concatenate([values[:, 0], values[:, 1]], axis=2)
+        values = values.reshape(subs * half, width)
         high_part, low_part = split(values)
         both = jnp.concatenate([high_part, low_part], axis=0).astype(BF16)
 
         def step(k, carry):
             at = pl.ds(pl.multiple_of(k * chunk, chunk), chunk)
-            key, unused = keys(index[:, at])
+            key, unused = keys(idx_buf[z, :, at])
             mask = lax.broadcasted_iota(jnp.int32, (half, chunk), 0) == key - half * slot
             picked = jnp.dot(both, own_low[:, at], preferred_element_type=F32)
             picked = picked[: subs * half] + picked[subs * half :]
@@ -220,19 +251,17 @@
     def return_step(t, carry):
         slots = (z + t, z - t)
         arrived = (z + t < n, z - t >= 0)
-        for way in range(2):
-            slot = slots[way]
-
-            @pl.when(arrived[way])
-            def _():
-                remote(
-                    table.at[slot], table.at[slot], tab_send.at[way, t], tab_recv.at[slot],
-                    sides[1 - way][1],
-                ).wait_recv()
-
-                @pl.when(sides[way][0])
+        for piece in range(pieces):
+            for way in range(2):
+                slot = slots[way]
+
+                @pl.when(arrived[way])
                 def _():
-                    table_copy(way, t, slot, table.at[slot]).start()
+                    table_copy(piece, way, t, slot, 1 - way).wait_recv()
+
+                    @pl.when(sides[way][0])
+                    def _():
+                        table_copy(piece, way, t, slot, way).start()
 
         for way in range(2):
             slot = slots[way]
@@ -256,9 +285,10 @@
         for way in range(2):
             @pl.when(sent[way] & sides[way][0])
             def _():
-                for arr in range(3):
-                    cell_copy(arr, way, t, slots[way], bufs[arr].at[slots[way]]).wait_send()
-                table_copy(way, t, slots[way], table.at[slots[way]]).wait_send()
+                for arr in range(len(spans)):
+                    cell_copy(arr, way, t, slots[way], way).wait_send()
+                for piece in range(pieces):
+                    table_copy(piece, way, t, slots[way], way).wait_send()
 
         return carry
 
@@ -272,41 +302,42 @@
     half = planes * rows // 2
     width = 2 * lanes
     assert planes % 2 == 0 and width & (width - 1) == 0
-    voxel = cell_voxel.reshape(blocks, cells // blocks)
-    line = voxel // lanes
-    key = line % half + half * block_dest
-    index = (key * width + voxel % lanes + lanes * (line // half)).reshape(1, cells)
-    chunk = 512
+    chunk = 2048
+    pieces = 4
     dma = pltpu.SemaphoreType.DMA
     vmem = pl.BlockSpec(memory_space=pltpu.VMEM)
-    return pl.pallas_call(
-        functools.partial(kernel, n, ny, chunk),
-        out_shape=(
-            jax.ShapeDtypeStruct(field.shape, F32),
-            jax.ShapeDtypeStruct(secrete.shape, F32),
-        ),
-        in_specs=[vmem, pl.BlockSpec(memory_space=pltpu.SMEM), vmem, vmem, vmem],
+    smem = pl.BlockSpec(memory_space=pltpu.SMEM)
+    anywhere = pl.BlockSpec(memory_space=pl.ANY)
+    flat = (subs * planes * rows, lanes)
+    updated, conc = pl.pallas_call(
+        functools.partial(kernel, n, ny, chunk, pieces),
+        out_shape=(pltpu.VMEM(flat, F32), pltpu.VMEM(secrete.shape, F32)),
+        in_specs=[anywhere, smem, anywhere, anywhere, anywhere, smem],
         out_specs=(vmem, vmem),
         scratch_shapes=[
+            pltpu.VMEM(field.shape, F32),
+            pltpu.VMEM((1, cells), jnp.int32),
             pltpu.VMEM((n, subs, cells), F32),
             pltpu.VMEM((n, subs, cells), F32),
             pltpu.VMEM((n, 1, cells), jnp.int32),
-            pltpu.VMEM((n,) + field.shape, F32),
+            pltpu.VMEM((n,) + flat, F32),
             pltpu.VMEM((subs, rows, lanes), F32),
             pltpu.VMEM((subs, rows, lanes), F32),
             pltpu.VMEM(field.shape, F32),
             pltpu.VMEM(field.shape, F32),
             pltpu.VMEM((4 * subs * half, width), F32),
             pltpu.VMEM((width, cells), BF16),
-            dma((2, n, 3)),
-            dma((n, 3)),
+            dma((4,)),
+            dma((2, n, 5)),
+            dma((n, 5)),
             dma((4,)),
             dma((4,)),
-            dma((2, n)),
-            dma((n,)),
+            dma((2, n, pieces)),
+            dma((n, pieces)),
         ],
         compiler_params=pltpu.CompilerParams(collective_id=0, has_side_effects=True),
-    )(field, diffusion, secrete, uptake, index)
+    )(field, diffusion, secrete, uptake, cell_voxel.reshape(1, cells), block_dest.reshape(blocks))
+    return updated.reshape(field.shape), conc
 
 
 def solution(mesh):

time: 39.7 us -> 30.7 us (0.77)
  Pallas kernels: 34.5 us -> 28.6 us
  other arithmetic: 2.05 us -> 0 us
  local copies, waits for them, and re-layouts: 2.14 us -> 1.26 us
    pallas_call x1, Pallas kernels: 34.5 us -> 28.6 us  [shards(): pl.pallas_call(functools.partial(kernel, n, ny, chunk, pieces), out_shape...]
    add x2 -> x0, other arithmetic: 2.05 us -> none  [the longest x1 1.4 us: shards(): key * width + voxel % lanes + lanes * (line // half)]
    unnamed x4 -> x2, local copies, waits for them, and re-layouts: 2.14 us -> 1.26 us
where the time goes in v2:
time: 30.7 us; the launch traced here: 30.5 us
  Pallas kernels  28.6 us (93%)
  local copies, waits for them, and re-layouts  1.26 us (4%)
  between operations  0.64 us (2%)
    pallas_call x1, Pallas kernels, shards(): pl.pallas_call(functools.partial(kernel, n, ny, chunk, pieces), out_shape...  28.6 us
    unnamed x2, local copies, waits for them, and re-layouts  1.26 us

profile of v2, /device:TPU:0, one launch (start us, length us, event | category | flops | bytes accessed | tf_op | source)
XLA Modules:
  0.0 30.5 jit_solution(10237349500343658301)
XLA Ops:
  0.6 28.6 %shard_map.77 = (f32[128,128]{1,0:T(8,128)S(1)}, f32[4,4096]{1,0:T(4,128)S(1)}) custom-call(f32[4,4,8,128]{3,2,1,0:T(8,128)} %field_in.1, f32[4]{0:T(128)} %diffusion.1, f32[4,4096]{1,0:T(4,128)} %secrete.1, f32[4,4096]{1,0:T(4,128)} %uptake.1, s32[1,4096]{1,0:T(1,128)} %bitcast.4, s32[32]{0:T(128)} %bitcast.5), custom_call_target="tpu_custom_call" | custom-call | tf_op jit(solution)/shard_map/pallas_call | solution.py:312
  29.2 0.6 %copy.10 = f32[4,4,8,128]{3,2,1,0:T(8,128)} copy(f32[4,4,8,128]{3,2,1,0:T(8,128)S(1)} %bitcast.3) | data formatting | bytes 131072
  29.8 0.6 %copy.11 = f32[4,4096]{1,0:T(4,128)} copy(f32[4,4096]{1,0:T(4,128)S(1)} %get-tuple-element.7) | data formatting | bytes 131072

commit v3 on v2

--- a/solution.py
+++ b/solution.py
@@ -19,9 +19,9 @@
 
 def kernel(
     n, ny, chunk, pieces,
-    field_in, diffusion, secrete, uptake, voxel_in, targets,
+    field_in, rates, secrete, uptake, voxel_in, targets_in,
     updated, conc,
-    field, voxel, sec_buf, upt_buf, idx_buf, table, z_low, z_high, y_low, y_high, acc, own_low,
+    diffusion, targets, field, voxel, sec_buf, upt_buf, idx_buf, table, z_low, z_high, y_low, y_high, acc, own_low,
     local_sem, send_sem, recv_sem, halo_send, halo_recv, tab_send, tab_recv,
 ):
     z = lax.axis_index("gz")
@@ -40,9 +40,9 @@
         pltpu.make_async_copy(secrete, sec_buf.at[z], local_sem.at[1]),
         pltpu.make_async_copy(uptake, upt_buf.at[z], local_sem.at[2]),
         pltpu.make_async_copy(field_in, field, local_sem.at[3]),
-    )
-    for load in loads:
-        load.start()
+        pltpu.make_async_copy(rates, diffusion, local_sem.at[4]),
+        pltpu.make_async_copy(targets_in, targets, local_sem.at[5]),
+    )
     barrier = pltpu.get_barrier_semaphore()
     sides = (
         (z > 0, {"gz": z - 1}),
@@ -54,8 +54,11 @@
         @pl.when(there)
         def _():
             pl.semaphore_signal(barrier, inc=1, device_id=device, device_id_type=MESH)
+    for load in loads:
+        load.start()
     acc[...] = jnp.zeros_like(acc)
     loads[0].wait()
+    loads[5].wait()
     for b in range(blocks):
         at = pl.ds(b * per_block, per_block)
         own = voxel[:, at]
@@ -63,7 +66,7 @@
         side = jnp.where(line_id >= half, 1, 0)
         key = line_id - half * side + half * targets[b]
         idx_buf[z, :, at] = key * width + (own & (lanes - 1)) + lanes * side
-    for load in loads[1:]:
+    for load in loads[1:5]:
         load.wait()
     pl.semaphore_wait(barrier, sum(jnp.where(there, 1, 0) for there, unused in sides))
 
@@ -93,12 +96,11 @@
             ref, ref, send_sem.at[way, step, arr], recv_sem.at[slot, arr], sides[side][1]
         )
 
-    def table_copy(piece, way, step, slot, side):
-        ref = table_ref(piece, slot)
-        src = updated.at[pl.ds(piece * depth, depth)] if step is None else ref
+    def table_copy(piece, way, dist, slot):
+        target = z + dist if way else z - dist
         return remote(
-            src, ref, tab_send.at[way, 0 if step is None else step, piece],
-            tab_recv.at[slot, piece], sides[side][1],
+            updated.at[pl.ds(piece * depth, depth)], table_ref(piece, slot),
+            tab_send.at[way, dist, piece], tab_recv.at[slot, piece], {"gz": target},
         )
 
     halo = (
@@ -216,11 +218,17 @@
 
             updated[pl.ds((s * planes + p) * rows, rows)] = (diffused + summed(0)) / (1.0 + summed(2))
 
-    for way in range(2):
-        @pl.when(sides[way][0])
-        def _():
-            for piece in range(pieces):
-                table_copy(piece, way, None, z, way).start()
+    def send_table(t, carry):
+        dist = n - t
+        for way in range(2):
+            @pl.when((z + dist < n) if way else (z - dist >= 0))
+            def _():
+                for piece in range(pieces):
+                    table_copy(piece, way, dist, z).start()
+
+        return carry
+
+    lax.fori_loop(1, n, send_table, 0)
 
     def look_up(tab, slot, first):
         values = tab[...].reshape(subs, 2, half, lanes)
@@ -251,23 +259,13 @@
     def return_step(t, carry):
         slots = (z + t, z - t)
         arrived = (z + t < n, z - t >= 0)
-        for piece in range(pieces):
-            for way in range(2):
-                slot = slots[way]
-
-                @pl.when(arrived[way])
-                def _():
-                    table_copy(piece, way, t, slot, 1 - way).wait_recv()
-
-                    @pl.when(sides[way][0])
-                    def _():
-                        table_copy(piece, way, t, slot, way).start()
-
         for way in range(2):
             slot = slots[way]
 
             @pl.when(arrived[way])
             def _():
+                for piece in range(pieces):
+                    table_copy(piece, way, t, slot).wait_recv()
                 look_up(table.at[slot], slot, False)
 
         return carry
@@ -287,8 +285,12 @@
             def _():
                 for arr in range(len(spans)):
                     cell_copy(arr, way, t, slots[way], way).wait_send()
+
+        for way in range(2):
+            @pl.when((t > 0) & ((z + t < n) if way else (z - t >= 0)))
+            def _():
                 for piece in range(pieces):
-                    table_copy(piece, way, t, slots[way], way).wait_send()
+                    table_copy(piece, way, t, z).wait_send()
 
         return carry
 
@@ -303,18 +305,19 @@
     width = 2 * lanes
     assert planes % 2 == 0 and width & (width - 1) == 0
     chunk = 2048
-    pieces = 4
+    pieces = 1
     dma = pltpu.SemaphoreType.DMA
     vmem = pl.BlockSpec(memory_space=pltpu.VMEM)
-    smem = pl.BlockSpec(memory_space=pltpu.SMEM)
     anywhere = pl.BlockSpec(memory_space=pl.ANY)
     flat = (subs * planes * rows, lanes)
     updated, conc = pl.pallas_call(
         functools.partial(kernel, n, ny, chunk, pieces),
         out_shape=(pltpu.VMEM(flat, F32), pltpu.VMEM(secrete.shape, F32)),
-        in_specs=[anywhere, smem, anywhere, anywhere, anywhere, smem],
+        in_specs=[anywhere] * 6,
         out_specs=(vmem, vmem),
         scratch_shapes=[
+            pltpu.SMEM((subs,), F32),
+            pltpu.SMEM((blocks,), jnp.int32),
             pltpu.VMEM(field.shape, F32),
             pltpu.VMEM((1, cells), jnp.int32),
             pltpu.VMEM((n, subs, cells), F32),
@@ -327,7 +330,7 @@
             pltpu.VMEM(field.shape, F32),
             pltpu.VMEM((4 * subs * half, width), F32),
             pltpu.VMEM((width, cells), BF16),
-            dma((4,)),
+            dma((6,)),
             dma((2, n, 5)),
             dma((n, 5)),
             dma((4,)),

time: 30.7 us -> 27.3 us (0.89)
  Pallas kernels: 28.6 us -> 25.1 us
    pallas_call x1, Pallas kernels: 28.6 us -> 25.1 us  [shards(): pl.pallas_call(functools.partial(kernel, n, ny, chunk, pieces), out_shape...]
where the time goes in v3:
time: 27.3 us; the launch traced here: 27 us
  Pallas kernels  25.1 us (92%)
  local copies, waits for them, and re-layouts  1.26 us (5%)
  between operations  0.64 us (2%)
    pallas_call x1, Pallas kernels, shards(): pl.pallas_call(functools.partial(kernel, n, ny, chunk, pieces), out_shape...  25.1 us
    unnamed x2, local copies, waits for them, and re-layouts  1.26 us

profile of v3, /device:TPU:0, one launch (start us, length us, event | category | flops | bytes accessed | tf_op | source)
XLA Modules:
  0.0 27.0 jit_solution(13961704230932663213)
XLA Ops:
  0.6 25.1 %shard_map.77 = (f32[128,128]{1,0:T(8,128)S(1)}, f32[4,4096]{1,0:T(4,128)S(1)}) custom-call(f32[4,4,8,128]{3,2,1,0:T(8,128)} %field_in.1, f32[4]{0:T(128)} %rates.1, f32[4,4096]{1,0:T(4,128)} %secrete.1, f32[4,4096]{1,0:T(4,128)} %uptake.1, s32[1,4096]{1,0:T(1,128)} %bitcast.4, s32[32]{0:T(128)} %bitcast.5), custom_call_target="tpu_custom_call" | custom-call | tf_op jit(solution)/shard_map/pallas_call | solution.py:313
  25.7 0.6 %copy.10 = f32[4,4,8,128]{3,2,1,0:T(8,128)} copy(f32[4,4,8,128]{3,2,1,0:T(8,128)S(1)} %bitcast.3) | data formatting | bytes 131072
  26.4 0.6 %copy.11 = f32[4,4096]{1,0:T(4,128)} copy(f32[4,4096]{1,0:T(4,128)S(1)} %get-tuple-element.7) | data formatting | bytes 131072

commit v4 on v3

--- a/solution.py
+++ b/solution.py
@@ -72,8 +72,8 @@
 
     part = cells // 2
     spans = (
-        (sec_buf, 0, part), (sec_buf, part, part), (idx_buf, 0, cells),
-        (upt_buf, 0, part), (upt_buf, part, part),
+        (sec_buf, 0, part), (idx_buf, 0, cells), (upt_buf, 0, part),
+        (sec_buf, part, part), (upt_buf, part, part),
     )
     depth = subs * area // pieces
 
@@ -124,7 +124,7 @@
     def keys(word):
         return lax.shift_right_logical(word, shift), word & (width - 1)
 
-    def deposit(idx, sec, upt, save):
+    def deposit(idx, sec, upt, save, first=0, last=cells):
         def step(k, carry):
             at = pl.ds(pl.multiple_of(k * chunk, chunk), chunk)
             key, low = keys(idx[:, at])
@@ -145,7 +145,7 @@
             )
             return carry
 
-        lax.fori_loop(0, cells // chunk, step, 0)
+        lax.fori_loop(first // chunk, last // chunk, step, 0)
 
     deposit(idx_buf.at[z], sec_buf.at[z], upt_buf.at[z], True)
 
@@ -163,12 +163,19 @@
                     @pl.when(sides[way][0])
                     def _():
                         cell_copy(arr, way, t, slot, way).start()
-        for way in range(2):
-            slot = slots[way]
-
-            @pl.when(arrived[way])
-            def _():
-                deposit(idx_buf.at[slot], sec_buf.at[slot], upt_buf.at[slot], False)
+
+            if arr not in (2, 4):
+                continue
+            first = 0 if arr == 2 else part
+            for way in range(2):
+                slot = slots[way]
+
+                @pl.when(arrived[way])
+                def _():
+                    deposit(
+                        idx_buf.at[slot], sec_buf.at[slot], upt_buf.at[slot], False,
+                        first, first + part,
+                    )
 
         return carry
 
@@ -256,21 +263,23 @@
 
     look_up(updated, z, True)
 
-    def return_step(t, carry):
-        slots = (z + t, z - t)
-        arrived = (z + t < n, z - t >= 0)
-        for way in range(2):
-            slot = slots[way]
-
-            @pl.when(arrived[way])
+    toward = jnp.where(2 * z < n, 1, -1)
+    for turn in (1, -1):
+        def return_step(t, carry):
+            slot = z + turn * toward * t
+
+            @pl.when((slot >= 0) & (slot < n))
             def _():
                 for piece in range(pieces):
-                    table_copy(piece, way, t, slot).wait_recv()
+                    remote(
+                        table_ref(piece, slot), table_ref(piece, slot), tab_send.at[0, t, piece],
+                        tab_recv.at[slot, piece], {"gz": slot},
+                    ).wait_recv()
                 look_up(table.at[slot], slot, False)
 
-        return carry
-
-    lax.fori_loop(1, n, return_step, 0)
+            return carry
+
+        lax.fori_loop(1, n, return_step, 0)
 
     for way in range(4):
         @pl.when(sides[way][0])

time: 27.3 us -> 26.1 us (0.956)
  Pallas kernels: 25.1 us -> 24 us
    pallas_call x1, Pallas kernels: 25.1 us -> 24 us  [shards(): pl.pallas_call(functools.partial(kernel, n, ny, chunk, pieces), out_shape...]
where the time goes in v4:
time: 26.1 us; the launch traced here: 25.9 us
  Pallas kernels  24 us (92%)
  local copies, waits for them, and re-layouts  1.26 us (5%)
  between operations  0.64 us (2%)
    pallas_call x1, Pallas kernels, shards(): pl.pallas_call(functools.partial(kernel, n, ny, chunk, pieces), out_shape...  24 us
    unnamed x2, local copies, waits for them, and re-layouts  1.26 us

profile of v4, /device:TPU:0, one launch (start us, length us, event | category | flops | bytes accessed | tf_op | source)
XLA Modules:
  0.0 25.9 jit_solution(11226660836639949632)
XLA Ops:
  0.6 24.0 %shard_map.77 = (f32[128,128]{1,0:T(8,128)S(1)}, f32[4,4096]{1,0:T(4,128)S(1)}) custom-call(f32[4,4,8,128]{3,2,1,0:T(8,128)} %field_in.1, f32[4]{0:T(128)} %rates.1, f32[4,4096]{1,0:T(4,128)} %secrete.1, f32[4,4096]{1,0:T(4,128)} %uptake.1, s32[1,4096]{1,0:T(1,128)} %bitcast.4, s32[32]{0:T(128)} %bitcast.5), custom_call_target="tpu_custom_call" | custom-call | tf_op jit(solution)/shard_map/pallas_call | solution.py:322
  24.6 0.6 %copy.10 = f32[4,4,8,128]{3,2,1,0:T(8,128)} copy(f32[4,4,8,128]{3,2,1,0:T(8,128)S(1)} %bitcast.3) | data formatting | bytes 131072
  25.2 0.6 %copy.11 = f32[4,4096]{1,0:T(4,128)} copy(f32[4,4096]{1,0:T(4,128)S(1)} %get-tuple-element.7) | data formatting | bytes 131072

commit v5 on v4

--- a/solution.py
+++ b/solution.py
@@ -72,8 +72,8 @@
 
     part = cells // 2
     spans = (
-        (sec_buf, 0, part), (idx_buf, 0, cells), (upt_buf, 0, part),
-        (sec_buf, part, part), (upt_buf, part, part),
+        (sec_buf, 0, part), (idx_buf, 0, part), (upt_buf, 0, part),
+        (idx_buf, part, part), (sec_buf, part, part), (upt_buf, part, part),
     )
     depth = subs * area // pieces
 
@@ -164,7 +164,7 @@
                     def _():
                         cell_copy(arr, way, t, slot, way).start()
 
-            if arr not in (2, 4):
+            if arr not in (2, 5):
                 continue
             first = 0 if arr == 2 else part
             for way in range(2):
@@ -340,8 +340,8 @@
             pltpu.VMEM((4 * subs * half, width), F32),
             pltpu.VMEM((width, cells), BF16),
             dma((6,)),
-            dma((2, n, 5)),
-            dma((n, 5)),
+            dma((2, n, 6)),
+            dma((n, 6)),
             dma((4,)),
             dma((4,)),
             dma((2, n, pieces)),

time: 26.1 us -> 25.5 us (0.977)
  Pallas kernels: 24 us -> 23.3 us
    pallas_call x1, Pallas kernels: 24 us -> 23.3 us  [shards(): pl.pallas_call(functools.partial(kernel, n, ny, chunk, pieces), out_shape...]
where the time goes in v5:
time: 25.5 us; the launch traced here: 25.2 us
  Pallas kernels  23.3 us (91%)
  local copies, waits for them, and re-layouts  1.26 us (5%)
  between operations  0.64 us (3%)
    pallas_call x1, Pallas kernels, shards(): pl.pallas_call(functools.partial(kernel, n, ny, chunk, pieces), out_shape...  23.3 us
    unnamed x2, local copies, waits for them, and re-layouts  1.26 us

profile of v5, /device:TPU:0, one launch (start us, length us, event | category | flops | bytes accessed | tf_op | source)
XLA Modules:
  0.0 25.2 jit_solution(17810349796145917976)
XLA Ops:
  0.6 23.3 %shard_map.77 = (f32[128,128]{1,0:T(8,128)S(1)}, f32[4,4096]{1,0:T(4,128)S(1)}) custom-call(f32[4,4,8,128]{3,2,1,0:T(8,128)} %field_in.1, f32[4]{0:T(128)} %rates.1, f32[4,4096]{1,0:T(4,128)} %secrete.1, f32[4,4096]{1,0:T(4,128)} %uptake.1, s32[1,4096]{1,0:T(1,128)} %bitcast.4, s32[32]{0:T(128)} %bitcast.5), custom_call_target="tpu_custom_call" | custom-call | tf_op jit(solution)/shard_map/pallas_call | solution.py:322
  23.9 0.6 %copy.10 = f32[4,4,8,128]{3,2,1,0:T(8,128)} copy(f32[4,4,8,128]{3,2,1,0:T(8,128)S(1)} %bitcast.3) | data formatting | bytes 131072
  24.6 0.6 %copy.11 = f32[4,4096]{1,0:T(4,128)} copy(f32[4,4096]{1,0:T(4,128)S(1)} %get-tuple-element.7) | data formatting | bytes 131072
